TPU v7x, 32 devices: a whole 2x2x4 slice. The times are simulated.
32 devices in a mesh: dp: 16 (over z, y, core), tensor: 2 (over x).
Axes of the slice: x: 2, y: 2, z: 4, core: 2. Of those that a mesh axis runs over, the one named last changes fastest.
Arguments:
- tokens: bfloat16 [32768, 768], P('dp'), may hold values from -6 to 6
- qkv_weight: bfloat16 [768, 3, 768], P(None, None, 'tensor'), may hold values from -0.21875 to 0.21875
- qv_bias: float32 [2, 768], P(None, 'tensor'), may hold values from -1.5 to 1.5
- proj_weight: bfloat16 [768, 768], P('tensor'), may hold values from -1.75 to 1.75
- proj_bias: float32 [768], replicated, may hold values from -1.5 to 1.5
- first_gain: float32 [768], replicated, may hold values from 0.5 to 1.5
- first_shift: float32 [768], replicated, may hold values from -1.5 to 1.5
- up_weight: bfloat16 [768, 3072], P(None, 'tensor'), may hold values from -0.21875 to 0.21875
- up_bias: float32 [3072], P('tensor'), may hold values from -1.5 to 1.5
- down_weight: bfloat16 [3072, 768], P('tensor'), may hold values from -0.109375 to 0.109375
- down_bias: float32 [768], replicated, may hold values from -1.5 to 1.5
- second_gain: float32 [768], replicated, may hold values from 0.5 to 1.5
- second_shift: float32 [768], replicated, may hold values from -1.5 to 1.5
- cotangent: bfloat16 [32768, 768], P('dp'), may hold values from -6 to 6
- bucket: int32 [16], P('dp'), may hold values from 0 to 1, as said below
- lengths: int32 [256], P('dp'), may hold values from 0 to 512, as said below
- dropped: int32 [256], P('dp'), may hold values 0 or 1
Outputs:
- result: bfloat16 [32768, 768], P('dp')
- tokens_grad: float32 [32768, 768], P('dp')
- qkv_weight_grad: float32 [768, 3, 768], P(None, None, 'tensor')
- qv_bias_grad: float32 [2, 768], P(None, 'tensor')
- proj_weight_grad: float32 [768, 768], P('tensor')
- proj_bias_grad: float32 [768], replicated
- first_gain_grad: float32 [768], replicated
- first_shift_grad: float32 [768], replicated
- up_weight_grad: float32 [768, 3072], P(None, 'tensor')
- up_bias_grad: float32 [3072], P('tensor')
- down_weight_grad: float32 [3072, 768], P('tensor')
- down_bias_grad: float32 [768], replicated
- second_gain_grad: float32 [768], replicated
- second_shift_grad: float32 [768], replicated
Inputs may be any that keep to these rules, and one draw needn't show every extreme that they name: Exactly a third of the token blocks, rounded down, have bucket 1. Slot k of block r (lengths[r * 16 + k]): in a block of bucket 1 every slot holds 32 to 128; in a block of bucket 0 slots k < 4 hold 128 to 512 and the other slots 0; in every block one used slot holds its whole span.
All inputs are finite; a program needn't handle non-finite values. No bound on the sum of `dropped` on one device may be relied on, other than what follows from the above.
Results may differ from a plain program's by a relative error of at most 0.015.
The roundings to bfloat16 on the way count: a program that leaves them out, or rounds other values in their place, can miss the bound.
Values may be sent and summed in bfloat16 or wider, within the bound.
No kernel may reach another device: no remote copies, remote signals or barrier semaphores. Data moves between devices by JAX's collectives and lax.ppermute only.
A program may use at most 192 MiB of HBM per device.

v0:
```python
import math

import jax
import jax.numpy as jnp
from jax import lax
from jax.sharding import PartitionSpec as P

HEAD = 64
LONG = 512
SHORT = 128


def dot_last(left, right):
    return lax.dot_general(
        left, right, (((1,), (1,)), ((), ())), preferred_element_type=jnp.float32
    )


def dot_first(left, right):
    return lax.dot_general(
        left, right, (((0,), (0,)), ((), ())), preferred_element_type=jnp.float32
    )


def layout(bucket, lengths, dropped, token_count):
    position = jnp.arange(token_count, dtype=jnp.int32)
    seq_span = jnp.where(bucket[0] == 1, SHORT, LONG).astype(jnp.int32)
    slot_index = position // seq_span
    offset = position % seq_span
    picker = slot_index[:, None] == jnp.arange(lengths.shape[0], dtype=jnp.int32)[None, :]
    token_length = jnp.sum(jnp.where(picker, lengths[None, :], 0), axis=1)
    token_drop = jnp.sum(jnp.where(picker, dropped[None, :], 0), axis=1)
    is_valid = offset < token_length
    keep_rows = is_valid & (token_drop == 0)
    block_count = token_count // LONG
    block_slot = slot_index.reshape(block_count, LONG)
    block_valid = is_valid.reshape(block_count, LONG)
    allowed = (block_slot[:, :, None] == block_slot[:, None, :]) & block_valid[:, None, :]
    return (keep_rows, allowed)


def norm_forward(values, gain_vec, shift_vec):
    centered = values - jnp.mean(values, axis=-1, keepdims=True)
    variance = jnp.mean(centered * centered, axis=-1, keepdims=True)
    inverse = lax.rsqrt(variance + 1e-05)
    scaled = centered * inverse
    return (scaled * gain_vec + shift_vec, scaled, inverse)


def norm_backward(upstream, scaled, inverse, gain_vec):
    gain_grad = jnp.sum(upstream * scaled, axis=0)
    shift_grad = jnp.sum(upstream, axis=0)
    through = upstream * gain_vec
    inner_part = (
        through
        - jnp.mean(through, axis=-1, keepdims=True)
        - scaled * jnp.mean(through * scaled, axis=-1, keepdims=True)
    )
    return (inner_part * inverse, gain_grad, shift_grad)


def gelu_slope(values):
    cumulative = 0.5 * (1.0 + lax.erf(values * (1.0 / math.sqrt(2.0))))
    density = jnp.exp(-0.5 * values * values) * (1.0 / math.sqrt(2.0 * math.pi))
    return cumulative + values * density


def block_scores(query_blk, key_blk, allowed_blk):
    row_count = query_blk.shape[0]
    head_split = (row_count, query_blk.shape[1] // HEAD, HEAD)
    scores = jnp.einsum(
        "qhd,khd->hqk",
        query_blk.reshape(head_split),
        key_blk.reshape(head_split),
        preferred_element_type=jnp.float32,
    ) * (1.0 / math.sqrt(HEAD))
    return (jnp.where(allowed_blk[None], scores, -1e30), head_split)


def attend_block(operands):
    query_blk, key_blk, value_blk, allowed_blk = operands
    scores, head_split = block_scores(query_blk, key_blk, allowed_blk)
    row_max = jnp.max(scores, axis=-1, keepdims=True)
    exp_scores = jnp.exp(scores - row_max)
    row_sum = jnp.sum(exp_scores, axis=-1, keepdims=True)
    prob_rows = exp_scores / row_sum
    context = jnp.einsum(
        "hqk,khd->qhd",
        prob_rows.astype(jnp.bfloat16),
        value_blk.reshape(head_split),
        preferred_element_type=jnp.float32,
    )
    context = context.reshape(query_blk.shape[0], -1).astype(jnp.bfloat16)
    log_total = row_max[..., 0] + jnp.log(row_sum[..., 0])
    return (context, log_total)


def attend_back(operands):
    query_blk, key_blk, value_blk, allowed_blk, log_total, grad_ctx = operands
    scores, head_split = block_scores(query_blk, key_blk, allowed_blk)
    prob_rows = jnp.exp(scores - log_total[..., None])
    prob_low = prob_rows.astype(jnp.bfloat16)
    grad_ctx_heads = grad_ctx.reshape(head_split)
    grad_prob = jnp.einsum(
        "qhd,khd->hqk",
        grad_ctx_heads,
        value_blk.reshape(head_split),
        preferred_element_type=jnp.float32,
    )
    row_dot = jnp.sum(prob_rows * grad_prob, axis=-1, keepdims=True)
    grad_score = (prob_rows * (grad_prob - row_dot)).astype(jnp.bfloat16)
    scale_factor = 1.0 / math.sqrt(HEAD)
    row_count = query_blk.shape[0]
    grad_query = (
        jnp.einsum(
            "hqk,khd->qhd",
            grad_score,
            key_blk.reshape(head_split),
            preferred_element_type=jnp.float32,
        )
        * scale_factor
    )
    grad_key = (
        jnp.einsum(
            "hqk,qhd->khd",
            grad_score,
            query_blk.reshape(head_split),
            preferred_element_type=jnp.float32,
        )
        * scale_factor
    )
    grad_value = jnp.einsum(
        "hqk,qhd->khd", prob_low, grad_ctx_heads, preferred_element_type=jnp.float32
    )
    return jnp.concatenate(
        [
            grad_query.reshape(row_count, -1).astype(jnp.bfloat16),
            grad_key.reshape(row_count, -1).astype(jnp.bfloat16),
            grad_value.reshape(row_count, -1).astype(jnp.bfloat16),
        ],
        axis=-1,
    )


def body(
    tokens,
    qkv_weight,
    qv_bias,
    proj_weight,
    proj_bias,
    first_gain,
    first_shift,
    up_weight,
    up_bias,
    down_weight,
    down_bias,
    second_gain,
    second_shift,
    cotangent,
    bucket,
    lengths,
    dropped,
):
    token_count, model_width = tokens.shape
    split_count = lax.axis_size("tensor")
    half_rows = token_count // split_count
    row_start = lax.axis_index("tensor") * half_rows
    block_count = token_count // LONG
    keep_rows, allowed = layout(bucket, lengths, dropped, token_count)
    local_width = qkv_weight.shape[2]
    qkv_flat = qkv_weight.reshape(model_width, 3 * local_width)
    projected = jnp.dot(tokens, qkv_flat, preferred_element_type=jnp.float32)
    bias_row = jnp.concatenate([qv_bias[0], jnp.zeros_like(qv_bias[0]), qv_bias[1]])
    qkv_low = (projected + bias_row).astype(jnp.bfloat16)
    block_view = (block_count, LONG, local_width)
    query_blocks = qkv_low[:, :local_width].reshape(block_view)
    key_blocks = qkv_low[:, local_width : 2 * local_width].reshape(block_view)
    value_blocks = qkv_low[:, 2 * local_width :].reshape(block_view)
    context, log_totals = lax.map(attend_block, (query_blocks, key_blocks, value_blocks, allowed))
    context = context.reshape(token_count, local_width)
    attn_share = lax.psum_scatter(
        jnp.dot(context, proj_weight, preferred_element_type=jnp.float32),
        "tensor",
        scatter_dimension=0,
        tiled=True,
    )
    own_tokens = lax.dynamic_slice_in_dim(tokens, row_start, half_rows, 0).astype(jnp.float32)
    first_sum = own_tokens + attn_share + proj_bias
    hidden, scaled_one, inverse_one = norm_forward(first_sum, first_gain, first_shift)
    hidden_all = lax.all_gather(hidden.astype(jnp.bfloat16), "tensor", axis=0, tiled=True)
    pre_act = jnp.dot(hidden_all, up_weight, preferred_element_type=jnp.float32) + up_bias
    activated = jax.nn.gelu(pre_act, approximate=False).astype(jnp.bfloat16)
    ffn_share = lax.psum_scatter(
        jnp.dot(activated, down_weight, preferred_element_type=jnp.float32).astype(jnp.bfloat16),
        "tensor",
        scatter_dimension=0,
        tiled=True,
    ).astype(jnp.float32)
    second_sum = hidden + ffn_share + down_bias
    normed, scaled_two, inverse_two = norm_forward(second_sum, second_gain, second_shift)
    keep_own = lax.dynamic_slice_in_dim(keep_rows, row_start, half_rows, 0)
    result_own = jnp.where(keep_own[:, None], normed, own_tokens).astype(jnp.bfloat16)
    result = lax.all_gather(result_own, "tensor", axis=0, tiled=True)
    upstream = lax.dynamic_slice_in_dim(cotangent, row_start, half_rows, 0).astype(jnp.float32)
    grad_normed = jnp.where(keep_own[:, None], upstream, 0.0)
    grad_skip = jnp.where(keep_own[:, None], 0.0, upstream)
    grad_second, gain_two_grad, shift_two_grad = norm_backward(
        grad_normed, scaled_two, inverse_two, second_gain
    )
    down_bias_grad = jnp.sum(grad_second, axis=0)
    branch_grad = lax.all_gather(grad_second.astype(jnp.bfloat16), "tensor", axis=0, tiled=True)
    down_grad = dot_first(activated, branch_grad)
    grad_act = dot_last(branch_grad, down_weight)
    grad_pre = (grad_act * gelu_slope(pre_act)).astype(jnp.bfloat16)
    up_bias_grad = jnp.sum(grad_pre, axis=0, dtype=jnp.float32)
    up_grad = dot_first(hidden_all, grad_pre)
    grad_hidden = grad_second + lax.psum_scatter(
        dot_last(grad_pre, up_weight).astype(jnp.bfloat16),
        "tensor",
        scatter_dimension=0,
        tiled=True,
    ).astype(jnp.float32)
    grad_first, gain_one_grad, shift_one_grad = norm_backward(
        grad_hidden, scaled_one, inverse_one, first_gain
    )
    proj_bias_grad = jnp.sum(grad_first, axis=0)
    attn_grad = lax.all_gather(grad_first.astype(jnp.bfloat16), "tensor", axis=0, tiled=True)
    proj_grad = dot_first(context, attn_grad)
    grad_ctx = dot_last(attn_grad, proj_weight).astype(jnp.bfloat16)
    grad_qkv = lax.map(
        attend_back,
        (query_blocks, key_blocks, value_blocks, allowed, log_totals, grad_ctx.reshape(block_view)),
    )
    grad_qkv = grad_qkv.reshape(token_count, 3 * local_width)
    qkv_grad = dot_first(tokens, grad_qkv).reshape(model_width, 3, local_width)
    qkv_sums = jnp.sum(grad_qkv, axis=0, dtype=jnp.float32).reshape(3, local_width)
    qv_bias_grad = jnp.stack([qkv_sums[0], qkv_sums[2]])
    grad_input_own = (
        grad_skip
        + grad_first
        + lax.psum_scatter(
            dot_last(grad_qkv, qkv_flat).astype(jnp.bfloat16),
            "tensor",
            scatter_dimension=0,
            tiled=True,
        ).astype(jnp.float32)
    )
    tokens_grad = lax.all_gather(
        grad_input_own.astype(jnp.bfloat16), "tensor", axis=0, tiled=True
    ).astype(grad_input_own.dtype)
    norm_sums = lax.psum(
        (
            proj_bias_grad,
            gain_one_grad,
            shift_one_grad,
            down_bias_grad,
            gain_two_grad,
            shift_two_grad,
        ),
        ("dp", "tensor"),
    )
    qkv_grad, qv_bias_grad, proj_grad, up_grad, up_bias_grad, down_grad = lax.psum(
        (qkv_grad, qv_bias_grad, proj_grad, up_grad, up_bias_grad, down_grad), "dp"
    )
    return (
        result,
        tokens_grad,
        qkv_grad,
        qv_bias_grad,
        proj_grad,
        norm_sums[0],
        norm_sums[1],
        norm_sums[2],
        up_grad,
        up_bias_grad,
        down_grad,
        norm_sums[3],
        norm_sums[4],
        norm_sums[5],
    )


def solution(mesh):
    placed = (
        P("dp", None),
        P(None, None, "tensor"),
        P(None, "tensor"),
        P("tensor", None),
        P(),
        P(),
        P(),
        P(None, "tensor"),
        P("tensor"),
        P("tensor", None),
        P(),
        P(),
        P(),
        P("dp", None),
        P("dp"),
        P("dp"),
        P("dp"),
    )
    return jax.shard_map(
        body,
        mesh=mesh,
        in_specs=placed,
        out_specs=(
            P("dp", None),
            P("dp", None),
            P(None, None, "tensor"),
            P(None, "tensor"),
            P("tensor", None),
            P(),
            P(),
            P(),
            P(None, "tensor"),
            P("tensor"),
            P("tensor", None),
            P(),
            P(),
            P(),
        ),
        check_vma=False,
    )
```

profile of v0, /device:TPU:0, one launch (start us, length us, event | category | flops | bytes accessed | tf_op | source)
XLA Modules:
  0.0 972.4 jit_solution(16050319743012541369)
XLA Ops:
  14.4 6.7 add_convert_fusion
  33.7 37.6 %while.22 = (s32[]{:T(128)}, bf16[4,512,384]{2,1,0:T(8,128)(2,1)}, f32[4,6,512]{2,1,0:T(8,128)}, bf16[4,512,384]{1,2,0:T(8,128)(2,1)}, pred[4,512,512]{1,2,0:T(8...) while((s32[]{:T(128)}, bf16[4,512,384]{2,1,0:T(8,128)(2,1)}, ...), condition=%wide.region_5.6_spmd, body=%wide.region_2.5_spmd.sunk | while | flops 421721088 | bytes 25792624 | solution.py:179
  71.3 6.0 fusion.72
  77.5 79.9 %reduce-scatter.5.cloned.1.call-done = f32[1024,768]{1,0:T(8,128)} async-done(((f32[2048,768]{1,0:T(8,128)}), f32[1024,768]{1,0:T(8,128)}) %reduce-scatter.5.cloned.1.call-update) | async-done | bytes 3145744 | tf_op jit(solution)/shard_map/reduce_scatter | solution.py:181
  163.6 45.0 %all-gather.6.cloned.1.call-done = bf16[2048,768]{1,0:T(8,128)(2,1)} async-done(((bf16[1024,768]{1,0:T(8,128)(2,1)}), bf16[2048,768]{1,0:T(8,128)(2,1)}) %all-gather.6.cloned.1.call-update) | async-done | bytes 3145744 | tf_op jit(solution)/shard_map/all_gather | solution.py:190
  208.6 33.2 %fusion.20 = (bf16[2048,1536]{1,0:T(8,128)(2,1)S(1)}, f32[2048,1536]{1,0:T(8,128)}) fusion(f32[1536]{0:T(1024)S(1)} %copy-done.29, bf16[2048,768]{1,0:T(8,128)(2,1)} %all-gather.6.cloned.1.call-done, bf16[768,1536]{1,0:T(8,128)(2,1)S(1)} %copy-done), kind=kOutput, calls=%fused_computation.40 | convolution fusion | flops 5039456256 | bytes 24385536 | tf_op jit(solution)/shard_map/dot_general | solution.py:191
  244.4 6.3 convolution_convert_fusion.2
  251.6 42.7 %reduce-scatter.7.cloned.1.call-done = bf16[1024,768]{1,0:T(8,128)(2,1)} async-done(((bf16[2048,768]{1,0:T(8,128)(2,1)}), bf16[1024,768]{1,0:T(8,128)(2,1)}) %reduce-scatter.7.cloned.1.call-update) | async-done | bytes 1572880 | tf_op jit(solution)/shard_map/reduce_scatter | solution.py:193
  306.3 45.0 %all-gather.10.cloned.1.call-done = bf16[2048,768]{1,0:T(8,128)(2,1)} async-done(((bf16[1024,768]{1,0:T(8,128)(2,1)}), bf16[2048,768]{1,0:T(8,128)(2,1)}) %all-gather.10.cloned.1.call-update) | async-done | bytes 3145744 | tf_op jit(solution)/shard_map/all_gather | solution.py:211
  351.3 12.6 %convert_reduce_fusion = (f32[1536]{0:T(1024)}, bf16[2048,1536]{1,0:T(8,128)(2,1)S(1)}) fusion(f32[2048,1536]{1,0:T(8,128)} %get-tuple-element.220, f32[1536]{0:T(1024)S(1)} %copy-done.29, bf16[2048,768]{1,0:T(8,128)(2,1)} %all-gather.10.cloned.1.call-done, bf16[1536,768]{1,0:T(8,128)(2,1)} %param.30), kind=kOutput, calls=%fused_computation.47 | convolution fusion | flops 4872731136 | bytes 24391680 | tf_op jit(solution)/shard_map/dot_general | solution.py:14
  366.6 6.4 convolution_convert_fusion.1
  373.1 43.5 %reduce-scatter.9.cloned.1.call-done = bf16[1024,768]{1,0:T(8,128)(2,1)} async-done(((bf16[2048,768]{1,0:T(8,128)(2,1)}), bf16[1024,768]{1,0:T(8,128)(2,1)}) %reduce-scatter.9.cloned.1.call-update) | async-done | bytes 1572880 | tf_op jit(solution)/shard_map/reduce_scatter | solution.py:217
  424.8 45.0 %all-gather.12.cloned.1.call-done = bf16[2048,768]{1,0:T(8,128)(2,1)} async-done(((bf16[1024,768]{1,0:T(8,128)(2,1)}), bf16[2048,768]{1,0:T(8,128)(2,1)}) %all-gather.12.cloned.1.call-update) | async-done | bytes 3145744 | tf_op jit(solution)/shard_map/all_gather | solution.py:227
  474.6 60.2 %while.23 = (s32[]{:T(128)}, bf16[4,512,1152]{1,2,0:T(8,128)(2,1)}, bf16[4,512,384]{1,2,0:T(8,128)(2,1)}, pred[4,512,512]{1,2,0:T(8,128)(4,1)}, bf16[4,512,384]{...) while((s32[]{:T(128)}, bf16[4,512,1152]{1,2,0:T(8,128)(2,1)}, ...), condition=%wide.region_19.20_spmd, body=%wide.region_17.19_spmd.sunk | while | flops 1034744832 | bytes 58806396 | solution.py:230
  534.8 6.7 copy.71
  541.6 7.9 convolution_convert_fusion
  550.4 42.7 %reduce-scatter.11.cloned.1.call-done = bf16[1024,768]{1,0:T(8,128)(2,1)} async-done(((bf16[2048,768]{1,0:T(8,128)(2,1)}), bf16[1024,768]{1,0:T(8,128)(2,1)}) %reduce-scatter.11.cloned.1.call-update) | async-done | bytes 1572880 | tf_op jit(solution)/shard_map/reduce_scatter | solution.py:241
  596.8 10.0 %fusion.76 = f32[1536,768]{1,0:T(8,128)} fusion(bf16[2048,1536]{1,0:T(8,128)(2,1)} %copy-done.30, bf16[2048,768]{1,0:T(8,128)(2,1)} %all-gather.10.cloned.1.call-done), kind=kOutput, calls=%fused_computation.151 | convolution fusion | flops 4831838208 | bytes 14155776 | tf_op jit(solution)/shard_map/dot_general | solution.py:20
  606.8 9.7 fusion.75
  628.4 11.2 %all-gather.8.cloned.1.call-done = bf16[2048,768]{1,0:T(8,128)(2,1)} async-done(((bf16[1024,768]{1,0:T(8,128)(2,1)}), bf16[2048,768]{1,0:T(8,128)(2,1)}) %all-gather.8.cloned.1.call-update) | async-done | bytes 3145744 | tf_op jit(solution)/shard_map/all_gather | solution.py:203
  639.6 40.4 %all-reduce = (f32[768]{0:T(1024)}, f32[768]{0:T(1024)}, f32[768]{0:T(1024)}, f32[768]{0:T(1024)}, f32[768]{0:T(1024)}, /*index=5*/f32[768]{0:T(1024)}) all-reduce(f32[768]{0:T(1024)S(1)} %get-tuple-element.197, f32[768]{0:T(1024)S(1)} %get-tuple-element.142, ...), channel_id=1, replica_groups=mesh['dp'=16,'tensor'=2] {'dp','tensor'}, use_global_device_ids=true, to_apply=%region_26.27 | all-reduce | flops 4608 | bytes 36864 | tf_op jit(solution)/shard_map/psum | solution.py:251
  683.0 63.2 %all-reduce.1 = (f32[2,384]{1,0:T(2,128)}, f32[1536]{0:T(1024)}) all-reduce(f32[2,384]{1,0:T(2,128)S(1)} %pad_maximum_fusion.1, f32[1536]{0:T(1024)S(1)} %copy-done.23), channel_id=1, replica_groups=mesh['dp'=16,'tensor'=2] {'dp'}, use_global_device_ids=true, to_apply=%region_23.24 | all-reduce | flops 2304 | bytes 18432 | tf_op jit(solution)/shard_map/psum | solution.py:262
  746.3 5.3 convert_element_type.130
  751.6 200.0 %all-reduce.5.cloned.1.call-done = (f32[768,3,384]{2,0,1:T(8,128)}, f32[384,768]{1,0:T(8,128)}, f32[768,1536]{1,0:T(8,128)}, f32[1536,768]{1,0:T(8,128)}) async-done(((f32[768,3,384]{2,0,1:T(8,128)}, f32[384,768]{1,0:T(8,128)}, f32[768,1536]{1,0:T(8,128)}, f32[1536,768]{1,0:T(8,128)}), (f32[768,3,384]{2,0,1:T(8,128)}, f32[384,768]{1,0:T(8,128)}, f32[768,1536]{1,0:T(8,128)}, ...) | async-done | bytes 14155792 | tf_op jit(solution)/shard_map/psum | solution.py:262
  (238 shorter events, 186.0 us)
Async XLA Ops:
  7.2 201.5 %copy-start = (bf16[768,1536]{1,0:T(8,128)(2,1)S(1)}, bf16[768,1536]{1,0:T(8,128)(2,1)}, u32[]{:S(2)}) copy-start(bf16[768,1536]{1,0:T(8,128)(2,1)} %param.28) | copy-start | bytes 7077892
  7.2 150.1 %reduce-scatter.5.cloned.1.call-start = ((), (), s32[]{:S(2)}) async-start(), calls=%async_computation.4 | async-start | bytes 9437184 | tf_op jit(solution)/shard_map/reduce_scatter | solution.py:181
  10.6 10.6 %copy-start.16 = (s32[2048]{0:T(1024)}, s32[2048]{0:T(1024)S(1)}, u32[]{:S(2)}) copy-start(s32[2048]{0:T(1024)S(1)} %get-tuple-element.152) | copy-start | bytes 24580
  77.4 80.0 %copy-start.24 = (f32[768]{0:T(1024)S(1)}, f32[768]{0:T(1024)}, u32[]{:S(2)}) copy-start(f32[768]{0:T(1024)} %param.25) | copy-start | bytes 9220
  77.4 131.2 %all-gather.6.cloned.1.call-start = ((), (), s32[]{:S(2)}) async-start(), calls=%async_computation.5 | async-start | bytes 4718592 | tf_op jit(solution)/shard_map/all_gather | solution.py:190
  161.8 46.8 %copy-start.29 = (f32[1536]{0:T(1024)S(1)}, f32[1536]{0:T(1024)}, u32[]{:S(2)}) copy-start(f32[1536]{0:T(1024)} %param.29) | copy-start | bytes 18436
  163.6 130.7 %reduce-scatter.7.cloned.1.call-start = ((), (), s32[]{:S(2)}) async-start(), calls=%async_computation.6 | async-start | bytes 4718592 | tf_op jit(solution)/shard_map/reduce_scatter | solution.py:193
  208.6 35.8 %copy-start.28 = (bf16[1536,768]{1,0:T(8,128)(2,1)S(1)}, bf16[1536,768]{1,0:T(8,128)(2,1)}, u32[]{:S(2)}) copy-start(bf16[1536,768]{1,0:T(8,128)(2,1)} %param.30) | copy-start | bytes 7077892
  250.8 43.5 %copy-start.25 = (f32[768]{0:T(1024)S(1)}, f32[768]{0:T(1024)}, u32[]{:S(2)}) copy-start(f32[768]{0:T(1024)} %param.31) | copy-start | bytes 9220
  250.8 100.5 %all-gather.10.cloned.1.call-start = ((), (), s32[]{:S(2)}) async-start(), calls=%async_computation.8 | async-start | bytes 4718592 | tf_op jit(solution)/shard_map/all_gather | solution.py:211
  306.2 110.4 %reduce-scatter.9.cloned.1.call-start = ((), (), s32[]{:S(2)}) async-start(), calls=%async_computation.9 | async-start | bytes 4718592 | tf_op jit(solution)/shard_map/reduce_scatter | solution.py:217
  373.1 43.5 %copy-start.3 = (f32[1024,768]{1,0:T(8,128)S(1)}, f32[1024,768]{1,0:T(8,128)}, u32[]{:S(2)}) copy-start(f32[1024,768]{1,0:T(8,128)} %copy-done.2) | copy-start | bytes 9437188
  373.1 96.7 %all-gather.12.cloned.1.call-start = ((), (), s32[]{:S(2)}) async-start(), calls=%async_computation.10 | async-start | bytes 4718592 | tf_op jit(solution)/shard_map/all_gather | solution.py:227
  423.4 46.4 %copy-start.14 = (bf16[384,768]{1,0:T(8,128)(2,1)S(1)}, bf16[384,768]{1,0:T(8,128)(2,1)}, u32[]{:S(2)}) copy-start(bf16[384,768]{1,0:T(8,128)(2,1)} %param.24) | copy-start | bytes 1769476
  424.7 168.3 %reduce-scatter.11.cloned.1.call-start = ((), (), s32[]{:S(2)}) async-start(), calls=%async_computation.11 | async-start | bytes 4718592 | tf_op jit(solution)/shard_map/reduce_scatter | solution.py:241
  549.5 43.5 %copy-start.5 = (f32[1024,768]{1,0:T(8,128)S(1)}, f32[1024,768]{1,0:T(8,128)}, u32[]{:S(2)}) copy-start(f32[1024,768]{1,0:T(8,128)} %copy-done.4) | copy-start | bytes 9437188
  549.6 90.0 %all-gather.8.cloned.1.call-start = ((), (), s32[]{:S(2)}) async-start(), calls=%async_computation.7 | async-start | bytes 4718592 | tf_op jit(solution)/shard_map/all_gather | solution.py:203
  550.3 196.0 %all-gather.14.cloned.1.call-start = ((), (), s32[]{:S(2)}) async-start(), calls=%async_computation.12 | async-start | bytes 4718592 | tf_op jit(solution)/shard_map/all_gather | solution.py:248
  596.8 354.9 %all-reduce.5.cloned.1.call-start = ((), (), s32[]{:S(2)}) async-start(), calls=%async_computation.13 | async-start | bytes 28311552 | tf_op jit(solution)/shard_map/psum | solution.py:262
  596.8 19.8 %slice-start.4 = ((s8[4718592]{0:T(1024)(128)(4,1)}), s8[4194304]{0:T(1024)(128)(4,1)S(1)}, s32[]{:S(2)}) async-start(s8[4718592]{0:T(1024)(128)(4,1)} %bitcast.156), calls=%async_computation.18 | async-start | bytes 8388608
  628.3 11.2 %copy-start.21 = (f32[768]{0:T(1024)S(1)}, f32[768]{0:T(1024)}, u32[]{:S(2)}) copy-start(f32[768]{0:T(1024)} %get-tuple-element.144) | copy-start | bytes 9220
  628.3 11.2 %copy-start.22 = (f32[768]{0:T(1024)S(1)}, f32[768]{0:T(1024)}, u32[]{:S(2)}) copy-start(f32[768]{0:T(1024)} %get-tuple-element.149) | copy-start | bytes 9220
  628.4 54.7 %copy-start.23 = (f32[1536]{0:T(1024)S(1)}, f32[1536]{0:T(1024)}, u32[]{:S(2)}) copy-start(f32[1536]{0:T(1024)} %get-tuple-element.221) | copy-start | bytes 18436
  746.3 205.3 %copy-start.9 = (bf16[2048,768]{1,0:T(8,128)(2,1)S(1)}, bf16[2048,768]{1,0:T(8,128)(2,1)}, u32[]{:S(2)}) copy-start(bf16[2048,768]{1,0:T(8,128)(2,1)} %all-gather.8.cloned.1.call-done) | copy-start | bytes 9437188
  (24 other events, 101.3 us)
Sparse Core Ops, SparseCore 0:
  77.5 79.7 reduce-scatter.4
  163.7 44.9 all-gather.5
  250.9 43.3 reduce-scatter.6
  306.3 44.9 all-gather.9
  373.2 43.3 reduce-scatter.8
  424.8 44.9 all-gather.11
  549.7 43.3 reduce-scatter.10
  594.6 44.9 all-gather.7
  641.7 45.8 all-gather.13
  692.5 259.0 all-reduce.4
where the time goes:
time: 982 us; the launch traced here: 972 us
  waiting for transfers between devices  556 us (57%)
  matrix products  152 us (15%)
  blocking collectives  104 us (11%)
  local copies, waits for them, and re-layouts  85.6 us (9%)
  other arithmetic  57.8 us (6%)
  between operations  15.8 us (2%)
    psum x1, waiting for transfers between devices, body(): lax.psum((qkv_grad, qv_bias_grad, proj_grad, up_grad, up_bias_grad, down_...  200 us
    reduce_scatter x1, waiting for transfers between devices, body(): lax.psum_scatter(jnp.dot(context, proj_weight, preferred_element_type=jnp...  79.9 us
    psum x1, blocking collectives, body(): lax.psum((qkv_grad, qv_bias_grad, proj_grad, up_grad, up_bias_grad, down_...  63.2 us
    all_gather x1, waiting for transfers between devices, body(): lax.all_gather(grad_second.astype(jnp.bfloat16), 'tensor', axis=0, tiled=...  45 us
    all_gather x1, waiting for transfers between devices, body(): lax.all_gather(grad_first.astype(jnp.bfloat16), 'tensor', axis=0, tiled=T...  45 us
    all_gather x1, waiting for transfers between devices, body(): lax.all_gather(hidden.astype(jnp.bfloat16), 'tensor', axis=0, tiled=True)  45 us
    reduce_scatter x1, waiting for transfers between devices, body(): lax.psum_scatter(dot_last(grad_pre, up_weight).astype(jnp.bfloat16), 'ten...  43.5 us
    reduce_scatter x1, waiting for transfers between devices, body(): lax.psum_scatter(dot_last(grad_qkv, qkv_flat).astype(jnp.bfloat16), 'tens...  42.7 us
  transfers between devices with their start and end apart: 10, of which 9 were waited for; matrix products, arithmetic and copies ran while one was open for 4% of the time, Pallas kernels for 0%

commit v1 on v0

v1 whole, which is shorter than its diff:
```python
import functools
import math

import jax
import jax.numpy as jnp
from jax import lax
from jax.experimental import pallas as pl
from jax.experimental.pallas import tpu as pltpu
from jax.sharding import PartitionSpec as P

HEAD = 64
LONG = 512
SHORT = 128
PAIR = 128
NEG = -1e30
BF = jnp.bfloat16
F32 = jnp.float32


def dot_nn(left, right):
    return lax.dot_general(left, right, (((1,), (0,)), ((), ())), preferred_element_type=F32)


def dot_nt(left, right):
    return lax.dot_general(left, right, (((1,), (1,)), ((), ())), preferred_element_type=F32)


def dot_tn(left, right):
    return lax.dot_general(left, right, (((0,), (0,)), ((), ())), preferred_element_type=F32)


def head_masks():
    lane = lax.broadcasted_iota(jnp.int32, (1, PAIR), 1)
    return (lane < HEAD, lane >= HEAD)


def only(mask, values):
    return jnp.where(mask, values, jnp.zeros_like(values))


def attend_tile(q, k, v, length):
    size = q.shape[0]
    valid = lax.broadcasted_iota(jnp.int32, (size, size), 0) < length
    total = None
    rows = []
    for mask in head_masks():
        scores = jnp.where(valid, dot_nt(k, only(mask, q)), NEG)
        top = jnp.max(scores, axis=0, keepdims=True)
        powers = jnp.exp(scores - top)
        summed = jnp.sum(powers, axis=0, keepdims=True)
        probs = (powers * (1.0 / summed)).astype(BF)
        part = dot_tn(probs, only(mask, v))
        total = part if total is None else total + part
        rows.append(top + jnp.log(summed))
    return total.astype(BF), jnp.concatenate(rows, axis=0)


def attend_kernel(info, q_ref, k_ref, v_ref, c_ref, lse_ref):
    block = pl.program_id(0)
    short = info[0] == 1

    @pl.when(jnp.logical_not(short))
    def _():
        c, rows = attend_tile(q_ref[...], k_ref[...], v_ref[...], info[1 + block])
        c_ref[...] = c
        lse_ref[0, 0] = rows

    @pl.when(short)
    def _():
        for sub in range(LONG // SHORT):
            at = slice(sub * SHORT, (sub + 1) * SHORT)
            length = info[1 + block * (LONG // SHORT) + sub]
            c, rows = attend_tile(q_ref[at, :], k_ref[at, :], v_ref[at, :], length)
            c_ref[at, :] = c
            lse_ref[0, 0, :, at] = rows


def attend_back_tile(q, k, v, grad_c, lse, length):
    size = q.shape[0]
    valid = lax.broadcasted_iota(jnp.int32, (size, size), 0) < length
    dq = dk = dv = None
    for index, mask in enumerate(head_masks()):
        q_own, c_own, k_own = only(mask, q), only(mask, grad_c), only(mask, k)
        scores = dot_nt(k, q_own)
        probs = jnp.where(valid, jnp.exp(scores - lse[index : index + 1, :]), 0.0)
        grad_probs = dot_nt(v, c_own)
        row_dot = jnp.sum(probs * grad_probs, axis=0, keepdims=True)
        grad_scores = (probs * (grad_probs - row_dot)).astype(BF)
        parts = (
            dot_tn(grad_scores, k_own),
            dot_nn(grad_scores, q_own),
            dot_nn(probs.astype(BF), c_own),
        )
        if dq is None:
            dq, dk, dv = parts
        else:
            dq, dk, dv = dq + parts[0], dk + parts[1], dv + parts[2]
    return (dq * (1.0 / math.sqrt(HEAD))).astype(BF), dk.astype(BF), dv.astype(BF)


def attend_back_kernel(info, q_ref, k_ref, v_ref, gc_ref, lse_ref, dq_ref, dk_ref, dv_ref):
    block = pl.program_id(0)
    short = info[0] == 1

    @pl.when(jnp.logical_not(short))
    def _():
        dq, dk, dv = attend_back_tile(
            q_ref[...], k_ref[...], v_ref[...], gc_ref[...], lse_ref[0, 0], info[1 + block]
        )
        dq_ref[...], dk_ref[...], dv_ref[...] = dq, dk, dv

    @pl.when(short)
    def _():
        for sub in range(LONG // SHORT):
            at = slice(sub * SHORT, (sub + 1) * SHORT)
            length = info[1 + block * (LONG // SHORT) + sub]
            dq, dk, dv = attend_back_tile(
                q_ref[at, :], k_ref[at, :], v_ref[at, :], gc_ref[at, :], lse_ref[0, 0, :, at], length
            )
            dq_ref[at, :], dk_ref[at, :], dv_ref[at, :] = dq, dk, dv


def attend_specs(width):
    pairs = width // PAIR
    return [
        pl.BlockSpec((LONG, PAIR), lambda b, p, info, k=k: (b, p + k * pairs)) for k in range(3)
    ]


def attend(info, qkv):
    rows, width = qkv.shape[0], qkv.shape[1] // 3
    blocks, pairs = rows // LONG, width // PAIR
    tile = pl.BlockSpec((LONG, PAIR), lambda b, p, info: (b, p))
    lse_tile = pl.BlockSpec((1, 1, 2, LONG), lambda b, p, info: (b, p, 0, 0))
    return pl.pallas_call(
        attend_kernel,
        grid_spec=pltpu.PrefetchScalarGridSpec(
            num_scalar_prefetch=1,
            grid=(blocks, pairs),
            in_specs=attend_specs(width),
            out_specs=[tile, lse_tile],
        ),
        out_shape=[
            jax.ShapeDtypeStruct((rows, width), BF),
            jax.ShapeDtypeStruct((blocks, pairs, 2, LONG), F32),
        ],
        compiler_params=pltpu.CompilerParams(vmem_limit_bytes=32 * 1024 * 1024),
        cost_estimate=pl.CostEstimate(
            flops=4 * rows * LONG * width, bytes_accessed=8 * rows * width, transcendentals=rows * LONG * width // HEAD
        ),
        name="attend",
    )(info, qkv, qkv, qkv)


def attend_back(info, qkv, grad_c, lse):
    rows, width = grad_c.shape
    blocks, pairs = rows // LONG, width // PAIR
    tile = pl.BlockSpec((LONG, PAIR), lambda b, p, info: (b, p))
    lse_tile = pl.BlockSpec((1, 1, 2, LONG), lambda b, p, info: (b, p, 0, 0))
    return pl.pallas_call(
        attend_back_kernel,
        grid_spec=pltpu.PrefetchScalarGridSpec(
            num_scalar_prefetch=1,
            grid=(blocks, pairs),
            in_specs=attend_specs(width) + [tile, lse_tile],
            out_specs=[tile] * 3,
        ),
        out_shape=[jax.ShapeDtypeStruct((rows, width), BF)] * 3,
        compiler_params=pltpu.CompilerParams(vmem_limit_bytes=48 * 1024 * 1024),
        cost_estimate=pl.CostEstimate(
            flops=10 * rows * LONG * width, bytes_accessed=14 * rows * width, transcendentals=rows * LONG * width // HEAD
        ),
        name="attend_back",
    )(info, qkv, qkv, qkv, grad_c, lse)


def swap_tensor(values):
    count = lax.axis_size("tensor")
    return lax.ppermute(values, "tensor", [(i, (i + 1) % count) for i in range(count)])


def swap_bit(values, bit):
    count = lax.axis_size("dp")
    return lax.ppermute(values, "dp", [(i, i ^ (1 << bit)) for i in range(count)])


def coordinate(bit):
    return (lax.axis_index("dp") >> bit) & 1


def half_of(values, which):
    rows = values.shape[0] // 2
    return lax.dynamic_slice_in_dim(values, which * rows, rows, 0)


def join(mine, other, bit):
    at = coordinate(bit)
    rows = mine.shape[0]
    whole = jnp.zeros((2 * rows,) + mine.shape[1:], mine.dtype)
    whole = lax.dynamic_update_slice_in_dim(whole, mine, at * rows, 0)
    return lax.dynamic_update_slice_in_dim(whole, other, (1 - at) * rows, 0)


def fetch(weight):
    mine = swap_tensor(half_of(weight, coordinate(0)))
    return join(mine, swap_bit(mine, 0), 0)


def scatter_step(values, bit):
    at = coordinate(bit)
    got = swap_bit(half_of(values, 1 - at).astype(BF), bit)
    return half_of(values, at).astype(F32) + got.astype(F32)


def dp_bits():
    return lax.axis_size("dp").bit_length() - 1


def sum_all(own, other):
    own, other = scatter_step(own, 0), scatter_step(other, 0)
    own = own + swap_tensor(other.astype(BF)).astype(F32)
    for bit in range(1, dp_bits()):
        own = scatter_step(own, bit)
    own = own.astype(BF)
    for bit in reversed(range(dp_bits())):
        own = join(own, swap_bit(own, bit), bit)
    return own.astype(F32)


def norm_forward(values, gain_vec, shift_vec):
    centered = values - jnp.mean(values, axis=-1, keepdims=True)
    variance = jnp.mean(centered * centered, axis=-1, keepdims=True)
    inverse = lax.rsqrt(variance + 1e-05)
    scaled = centered * inverse
    return (scaled * gain_vec + shift_vec, scaled, inverse)


def norm_backward(upstream, scaled, inverse, gain_vec):
    gain_grad = jnp.sum(upstream * scaled, axis=0)
    shift_grad = jnp.sum(upstream, axis=0)
    through = upstream * gain_vec
    inner_part = (
        through
        - jnp.mean(through, axis=-1, keepdims=True)
        - scaled * jnp.mean(through * scaled, axis=-1, keepdims=True)
    )
    return (inner_part * inverse, gain_grad, shift_grad)


def gelu_slope(values):
    cumulative = 0.5 * (1.0 + lax.erf(values * (1.0 / math.sqrt(2.0))))
    density = jnp.exp(-0.5 * values * values) * (1.0 / math.sqrt(2.0 * math.pi))
    return cumulative + values * density


def kept_rows(bucket, lengths, dropped, start, count):
    position = start + jnp.arange(count, dtype=jnp.int32)
    span = jnp.where(bucket[0] == 1, SHORT, LONG).astype(jnp.int32)
    slot, offset = position // span, position % span
    picker = slot[:, None] == jnp.arange(lengths.shape[0], dtype=jnp.int32)[None, :]
    limit = jnp.where(dropped == 0, lengths, 0)
    return offset < jnp.sum(jnp.where(picker, limit[None, :], 0), axis=1)


def body(
    tokens,
    qkv_weight,
    qv_bias,
    proj_weight,
    proj_bias,
    first_gain,
    first_shift,
    up_weight,
    up_bias,
    down_weight,
    down_bias,
    second_gain,
    second_shift,
    cotangent,
    bucket,
    lengths,
    dropped,
):
    token_count, width = tokens.shape
    parts = lax.axis_size("tensor")
    rows = token_count // parts
    place = lax.axis_index("tensor")
    row_start = place * rows
    local = qkv_weight.shape[2]
    keep = kept_rows(bucket, lengths, dropped, row_start, rows)[:, None]
    slots = rows // SHORT
    first_slot = jnp.where(bucket[0] == 1, place * slots, place * (rows // LONG))
    info = jnp.concatenate([bucket, lax.dynamic_slice_in_dim(lengths, first_slot, slots, 0)])
    x_low = lax.dynamic_slice_in_dim(tokens, row_start, rows, 0)
    x = x_low.astype(F32)
    upstream = lax.dynamic_slice_in_dim(cotangent, row_start, rows, 0).astype(F32)

    qkv_own = qkv_weight.reshape(width, 3 * local)
    qkv_oth = fetch(qkv_own)
    proj_oth = fetch(proj_weight)
    up_oth = fetch(up_weight)
    down_oth = fetch(down_weight)
    qv_bias_oth = swap_tensor(qv_bias)
    up_bias_oth = swap_tensor(up_bias)
    halves = range(2)
    qkv_w, proj_w = (qkv_own, qkv_oth), (proj_weight, proj_oth)
    up_w, down_w = (up_weight, up_oth), (down_weight, down_oth)
    qv_b, up_b = (qv_bias, qv_bias_oth), (up_bias, up_bias_oth)

    scale = 1.0 / math.sqrt(HEAD)
    qkv, context, lse = [], [], []
    for h in halves:
        bias_row = jnp.concatenate([qv_b[h][0], jnp.zeros_like(qv_b[h][0]), qv_b[h][1]])
        factor = jnp.concatenate([jnp.full((local,), scale, F32), jnp.ones((2 * local,), F32)])
        qkv.append(((dot_nn(x_low, qkv_w[h]) + bias_row) * factor).astype(BF))
        c, rows_lse = attend(info, qkv[h])
        context.append(c)
        lse.append(rows_lse)
    first_sum = x + proj_bias + (dot_nn(context[0], proj_w[0]) + dot_nn(context[1], proj_w[1]))
    hidden, scaled_one, inverse_one = norm_forward(first_sum, first_gain, first_shift)
    hidden_low = hidden.astype(BF)
    pre_act = [dot_nn(hidden_low, up_w[h]) + up_b[h] for h in halves]
    activated = [jax.nn.gelu(pre_act[h], approximate=False).astype(BF) for h in halves]
    second_sum = hidden + down_bias + (dot_nn(activated[0], down_w[0]) + dot_nn(activated[1], down_w[1]))
    normed, scaled_two, inverse_two = norm_forward(second_sum, second_gain, second_shift)
    result_own = jnp.where(keep, normed, x).astype(BF)

    def both_rows(mine):
        other = swap_tensor(mine)
        whole = jnp.zeros((token_count, width), mine.dtype)
        whole = lax.dynamic_update_slice_in_dim(whole, mine, row_start, 0)
        return lax.dynamic_update_slice_in_dim(whole, other, rows - row_start, 0)

    result = both_rows(result_own)

    grad_normed = jnp.where(keep, upstream, 0.0)
    grad_skip = jnp.where(keep, 0.0, upstream)
    grad_second, gain_two_grad, shift_two_grad = norm_backward(
        grad_normed, scaled_two, inverse_two, second_gain
    )
    down_bias_grad = jnp.sum(grad_second, axis=0)
    branch_grad = grad_second.astype(BF)
    down_grad = [dot_tn(activated[h], branch_grad) for h in halves]
    down_total = sum_all(*down_grad)
    grad_pre = [
        (dot_nt(branch_grad, down_w[h]) * gelu_slope(pre_act[h])).astype(BF) for h in halves
    ]
    up_grad = [dot_tn(hidden_low, grad_pre[h]) for h in halves]
    up_bias_grad = [jnp.sum(grad_pre[h], axis=0, dtype=F32) for h in halves]
    up_total = sum_all(*up_grad)
    grad_hidden = grad_second + (dot_nt(grad_pre[0], up_w[0]) + dot_nt(grad_pre[1], up_w[1]))
    grad_first, gain_one_grad, shift_one_grad = norm_backward(
        grad_hidden, scaled_one, inverse_one, first_gain
    )
    proj_bias_grad = jnp.sum(grad_first, axis=0)
    attn_grad = grad_first.astype(BF)
    proj_grad = [dot_tn(context[h], attn_grad) for h in halves]
    qkv_grad, qv_sums, input_grad = [], [], grad_skip + grad_first
    for h in halves:
        grad_ctx = dot_nt(attn_grad, proj_w[h]).astype(BF)
        dq, dk, dv = attend_back(info, qkv[h], grad_ctx, lse[h])
        grads = jnp.concatenate([dq, dk, dv], axis=1)
        qkv_grad.append(dot_tn(x_low, grads))
        qv_sums.append(jnp.stack([jnp.sum(dq, axis=0, dtype=F32), jnp.sum(dv, axis=0, dtype=F32)]))
        input_grad = input_grad + dot_nt(grads, qkv_w[h])
    qkv_total = sum_all(*qkv_grad)
    proj_total = sum_all(*proj_grad)
    tokens_grad = both_rows(input_grad.astype(BF)).astype(F32)

    norm_sums = lax.psum(
        jnp.stack(
            [proj_bias_grad, gain_one_grad, shift_one_grad, down_bias_grad, gain_two_grad, shift_two_grad]
        ),
        ("dp", "tensor"),
    )
    bias_own = jnp.concatenate([qv_sums[0].reshape(-1), up_bias_grad[0]])
    bias_oth = jnp.concatenate([qv_sums[1].reshape(-1), up_bias_grad[1]])
    bias_sum = lax.psum(bias_own + swap_tensor(bias_oth), "dp")
    return (
        result,
        tokens_grad,
        qkv_total.reshape(width, 3, local),
        bias_sum[: 2 * local].reshape(2, local),
        proj_total,
        norm_sums[0],
        norm_sums[1],
        norm_sums[2],
        up_total,
        bias_sum[2 * local :],
        down_total,
        norm_sums[3],
        norm_sums[4],
        norm_sums[5],
    )


def solution(mesh):
    rows, columns, whole = P("dp", None), P(None, "tensor"), P()
    return jax.shard_map(
        body,
        mesh=mesh,
        in_specs=(
            rows,
            P(None, None, "tensor"),
            columns,
            P("tensor", None),
            whole,
            whole,
            whole,
            columns,
            P("tensor"),
            P("tensor", None),
            whole,
            whole,
            whole,
            rows,
            P("dp"),
            P("dp"),
            P("dp"),
        ),
        out_specs=(
            rows,
            rows,
            P(None, None, "tensor"),
            columns,
            P("tensor", None),
            whole,
            whole,
            whole,
            columns,
            P("tensor"),
            P("tensor", None),
            whole,
            whole,
            whole,
        ),
        check_vma=False,
    )
```

time: 982 us -> 655 us (0.67)
  waiting for transfers between devices: 556 us -> 161 us
  local copies, waits for them, and re-layouts: 85.6 us -> 131 us
  Pallas kernels: 0 us -> 40.5 us
  starting transfers between devices: 0.41 us -> 38.6 us
  matrix products: 152 us -> 115 us
  other arithmetic: 57.8 us -> 33.5 us
  blocking collectives: 104 us -> 123 us
  between operations: 15.8 us -> 3.06 us
    reduce_scatter x4 -> x0, waiting for transfers between devices: 209 us -> none  [the longest x1 79.9 us: body(): lax.psum_scatter(jnp.dot(context, proj_weight, preferred_element_type=jnp...]
    psum x1 -> x0, waiting for transfers between devices: 200 us -> none  [body(): lax.psum((qkv_grad, qv_bias_grad, proj_grad, up_grad, up_bias_grad, down_...]
    ppermute x0 -> x53, waiting for transfers between devices: none -> 161 us  [the longest x13 90.2 us: swap_tensor(): lax.ppermute(values, 'tensor', [(i, (i + 1) % count) for i in range(count)])]
    all_gather x5 -> x0, waiting for transfers between devices: 146 us -> none  [the longest x1 45 us: body(): lax.all_gather(grad_second.astype(jnp.bfloat16), 'tensor', axis=0, tiled=...]
    dynamic_update_slice x8 -> x42, local copies, waits for them, and re-layouts: 4.05 us -> 58.9 us  [the longest x21 31.4 us: join(): return lax.dynamic_update_slice_in_dim(whole, other, (1 - at) * rows, 0)]
    pallas_call x0 -> x4, Pallas kernels: none -> 40.5 us  [the longest x2 22 us: attend_back(): pl.pallas_call(attend_back_kernel, grid_spec=pltpu.PrefetchScalarGridSpec...]
    ppermute x0 -> x53, starting transfers between devices: none -> 38.6 us  [the longest x40 22 us: swap_bit(): return lax.ppermute(values, 'dp', [(i, i ^ 1 << bit) for i in range(count)])]
    dot_general x40 -> x24, matrix products: 152 us -> 115 us  [the longest x8 55.7 us: dot_nn(): lax.dot_general(left, right, (((1,), (0,)), ((), ())), preferred_element_...]
  transfers between devices with their start and end apart: 10 -> 53, of which waited for: 9 -> 19; matrix products, arithmetic and copies ran while one was open for 4% -> 28% of each run, Pallas kernels for 0% -> 3%
where the time goes in v1:
time: 655 us; the launch traced here: 645 us
  waiting for transfers between devices  161 us (25%)
  local copies, waits for them, and re-layouts  131 us (20%)
  blocking collectives  123 us (19%)
  matrix products  115 us (18%)
  Pallas kernels  40.5 us (6%)
  starting transfers between devices  38.6 us (6%)
  other arithmetic  33.5 us (5%)
    ppermute x13, waiting for transfers between devices, swap_tensor(): lax.ppermute(values, 'tensor', [(i, (i + 1) % count) for i in range(count)])  90.2 us
    ppermute x40, waiting for transfers between devices, swap_bit(): return lax.ppermute(values, 'dp', [(i, i ^ 1 << bit) for i in range(count)])  70.8 us
    psum x1, blocking collectives, body(): lax.psum(jnp.stack([proj_bias_grad, gain_one_grad, shift_one_grad, down_b...  64.9 us
    psum x1, blocking collectives, body(): bias_sum = lax.psum(bias_own + swap_tensor(bias_oth), 'dp')  57.8 us
    dot_general x8, matrix products, dot_nn(): lax.dot_general(left, right, (((1,), (0,)), ((), ())), preferred_element_...  55.7 us
    dynamic_update_slice x21, local copies, waits for them, and re-layouts, join(): return lax.dynamic_update_slice_in_dim(whole, other, (1 - at) * rows, 0)  31.4 us
    dot_general x8, matrix products, dot_nt(): lax.dot_general(left, right, (((1,), (1,)), ((), ())), preferred_element_...  30.2 us
    dot_general x8, matrix products, dot_tn(): lax.dot_general(left, right, (((0,), (0,)), ((), ())), preferred_element_...  28.8 us
  transfers between devices with their start and end apart: 53, of which 19 were waited for; matrix products, arithmetic and copies ran while one was open for 28% of the time, Pallas kernels for 3%

profile of v1, /device:TPU:0, one launch (start us, length us, event | category | flops | bytes accessed | tf_op | source)
XLA Modules:
  0.0 645.2 jit_solution(5882093740203627550)
XLA Ops:
  36.5 9.1 %attend.2 = (bf16[1024,384]{1,0:T(8,128)(2,1)S(1)}, f32[2,3,2,512]{3,2,1,0:T(2,128)S(1)}) custom-call(s32[9]{0:T(128)S(1)} %pad_add_fusion.info, bf16[1024,1152]{1,0:T(8,128)(2,1)S(1)} %multiply_convert_fusion.1.q_ref.k_ref.v_ref, bf16[1024,1152]{1,0:T(8,128)(2,1)S(1)} %multiply_convert_fusion.1.q_ref.k_ref.v_ref, ...), custom_call_target="tpu_custom_call" | custom-call | flops 805306368 | bytes 3145728 | tf_op jit(solution)/shard_map/attend/pallas_call | solution.py:135
  49.1 13.2 %collective-permute-done.5 = bf16[384,1536]{1,0:T(8,128)(2,1)} collective-permute-done((bf16[384,1536]{1,0:T(8,128)(2,1)}, bf16[384,1536]{1,0:T(8,128)(2,1)}, u32[]{:S(2)}, u32[]{:S(2)}) %collective-permute-start.5) | collective-permute-done | bytes 1179680 | tf_op jit(solution)/shard_map/ppermute | solution.py:179
  62.3 24.5 %collective-permute-done.8 = bf16[768,768]{1,0:T(8,128)(2,1)S(1)} collective-permute-done((bf16[768,768]{1,0:T(8,128)(2,1)}, bf16[768,768]{1,0:T(8,128)(2,1)S(1)}, u32[]{:S(2)}, u32[]{:S(2)}) %collective-permute-start.8) | collective-permute-done | bytes 1179680 | tf_op jit(solution)/shard_map/ppermute | solution.py:179
  92.4 9.3 %attend.3 = (bf16[1024,384]{1,0:T(8,128)(2,1)S(1)}, f32[2,3,2,512]{3,2,1,0:T(2,128)S(1)}) custom-call(s32[9]{0:T(128)S(1)} %pad_add_fusion.info, bf16[1024,1152]{1,0:T(8,128)(2,1)S(1)} %multiply_convert_fusion.q_ref.k_ref.v_ref, bf16[1024,1152]{1,0:T(8,128)(2,1)S(1)} %multiply_convert_fusion.q_ref.k_ref.v_ref, ...), custom_call_target="tpu_custom_call" | custom-call | flops 805306368 | bytes 3145728 | tf_op jit(solution)/shard_map/attend/pallas_call | solution.py:135
  105.1 18.3 %fusion.2 = (bf16[1024,1536]{1,0:T(8,128)(2,1)S(1)}, f32[1024,1536]{1,0:T(8,128)}) fusion(f32[1536]{0:T(1024)S(1)} %copy-done.44, bf16[1024,768]{0,1:T(8,128)(2,1)S(1)} %fusion.48, bf16[768,1536]{1,0:T(8,128)(2,1)S(1)} %copy-done.37), kind=kOutput, calls=%fused_computation.6 | convolution fusion | flops 2519728128 | bytes 13375488 | tf_op jit(solution)/shard_map/dot_general | solution.py:21
  127.9 18.4 %fusion.5 = (bf16[1024,1536]{1,0:T(8,128)(2,1)}, f32[1024,1536]{1,0:T(8,128)}) fusion(f32[1536]{0:T(1024)S(1)} %collective-permute-done.7, bf16[1024,768]{0,1:T(8,128)(2,1)S(1)} %fusion.48, bf16[768,1536]{1,0:T(8,128)(2,1)S(1)} %constant_dynamic-update-slice_fusion.32), kind=kOutput, calls=%fused_computation.9 | convolution fusion | flops 2519728128 | bytes 13375488 | tf_op jit(solution)/shard_map/dot_general | solution.py:21
  146.5 6.3 fusion.61
  166.6 5.9 convert_reduce_fusion.1
  181.0 7.4 %convert_reduce_fusion = (f32[1536]{0:T(1024)S(1)}, bf16[1024,1536]{1,0:T(8,128)(2,1)S(1)}) fusion(f32[1024,1536]{1,0:T(8,128)} %get-tuple-element.112, f32[1536]{0:T(1024)S(1)} %collective-permute-done.7, bf16[1024,768]{0,1:T(8,128)(2,1)S(1)} %get-tuple-element.103, bf16[1536,768]{1,0:T(8,128)(2,1)S(1)} %constant_dynamic-update-slice_fusion.30), kind=kOutput, calls=%fused_computation.22 | convolution fusion | flops 2436364800 | bytes 13381632 | tf_op jit(solution)/shard_map/dot_general | solution.py:25
  205.7 10.8 %attend_back.3 = (bf16[1024,384]{1,0:T(8,128)(2,1)S(1)}, bf16[1024,384]{1,0:T(8,128)(2,1)S(1)}, bf16[1024,384]{1,0:T(8,128)(2,1)S(1)}) custom-call(s32[9]{0:T(128)S(1)} %pad_add_fusion.info, bf16[1024,1152]{1,0:T(8,128)(2,1)S(1)} %copy-done.5, bf16[1024,1152]{1,0:T(8,128)(2,1)S(1)} %copy-done.5, bf16[1024,1152]{1,0:T(8,128)(2,1)S(1)} %copy-done.5, ...), custom_call_target="tpu_custom_call" | custom-call | flops 2013265920 | bytes 5505024 | tf_op jit(solution)/shard_map/attend_back/pallas_call | solution.py:160
  216.7 11.2 %attend_back.2 = (bf16[1024,384]{1,0:T(8,128)(2,1)S(1)}, bf16[1024,384]{1,0:T(8,128)(2,1)S(1)}, bf16[1024,384]{1,0:T(8,128)(2,1)S(1)}) custom-call(s32[9]{0:T(128)S(1)} %pad_add_fusion.info, bf16[1024,1152]{1,0:T(8,128)(2,1)S(1)} %copy-done.3, bf16[1024,1152]{1,0:T(8,128)(2,1)S(1)} %copy-done.3, bf16[1024,1152]{1,0:T(8,128)(2,1)S(1)} %copy-done.3, ...), custom_call_target="tpu_custom_call" | custom-call | flops 2013265920 | bytes 5505024 | tf_op jit(solution)/shard_map/attend_back/pallas_call | solution.py:160
  271.1 64.9 %psum.15 = f32[6,768]{1,0:T(8,128)S(1)} all-reduce(f32[6,768]{1,0:T(8,128)S(1)} %stack.51), channel_id=1, replica_groups=mesh['dp'=16,'tensor'=2] {'dp','tensor'}, use_global_device_ids=true, to_apply=%region_22.23 | all-reduce | flops 4608 | bytes 36864 | tf_op jit(solution)/shard_map/psum | solution.py:370
  366.8 15.1 %collective-permute-done.22 = f32[2304]{0:T(1024)S(1)} collective-permute-done((f32[2304]{0:T(1024)S(1)}, f32[2304]{0:T(1024)S(1)}, u32[]{:S(2)}, u32[]{:S(2)}) %collective-permute-start.22) | collective-permute-done | bytes 9248 | tf_op jit(solution)/shard_map/ppermute | solution.py:179
  383.5 57.8 %psum.14 = f32[2304]{0:T(1024)S(1)} all-reduce(f32[2304]{0:T(1024)S(1)} %maximum_add_fusion), channel_id=1, replica_groups=mesh['dp'=16,'tensor'=2] {'dp'}, use_global_device_ids=true, to_apply=%region_15.16 | all-reduce | flops 2304 | bytes 18432 | tf_op jit(solution)/shard_map/psum | solution.py:378
  450.8 10.2 %collective-permute-done.15 = bf16[192,1152]{1,0:T(8,128)(2,1)S(1)} collective-permute-done((bf16[192,1152]{1,0:T(8,128)(2,1)S(1)}, bf16[192,1152]{1,0:T(8,128)(2,1)S(1)}, u32[]{:S(2)}, u32[]{:S(2)}) %collective-permute-start.15) | collective-permute-done | bytes 442400 | tf_op jit(solution)/shard_map/ppermute | solution.py:184
  463.2 11.3 %collective-permute-done.45 = bf16[768,768]{1,0:T(8,128)(2,1)S(1)} collective-permute-done((bf16[768,768]{1,0:T(8,128)(2,1)S(1)}, bf16[768,768]{1,0:T(8,128)(2,1)S(1)}, u32[]{:S(2)}, u32[]{:S(2)}) %collective-permute-start.45) | collective-permute-done | bytes 1179680 | tf_op jit(solution)/shard_map/ppermute | solution.py:179
  475.8 24.0 %collective-permute-done.35 = bf16[384,1536]{1,0:T(8,128)(2,1)S(1)} collective-permute-done((bf16[384,1536]{1,0:T(8,128)(2,1)S(1)}, bf16[384,1536]{1,0:T(8,128)(2,1)S(1)}, u32[]{:S(2)}, u32[]{:S(2)}) %collective-permute-start.35) | collective-permute-done | bytes 1179680 | tf_op jit(solution)/shard_map/ppermute | solution.py:179
  502.6 5.3 collective-permute-done.17
  522.8 11.4 %collective-permute-done.47 = bf16[192,768]{1,0:T(8,128)(2,1)S(1)} collective-permute-done((bf16[192,768]{1,0:T(8,128)(2,1)S(1)}, bf16[192,768]{1,0:T(8,128)(2,1)S(1)}, u32[]{:S(2)}, u32[]{:S(2)}) %collective-permute-start.47) | collective-permute-done | bytes 294944 | tf_op jit(solution)/shard_map/ppermute | solution.py:184
  534.6 8.3 %collective-permute-done.37 = bf16[96,1536]{1,0:T(8,128)(2,1)S(1)} collective-permute-done((bf16[96,1536]{1,0:T(8,128)(2,1)S(1)}, bf16[96,1536]{1,0:T(8,128)(2,1)S(1)}, u32[]{:S(2)}, u32[]{:S(2)}) %collective-permute-start.37) | collective-permute-done | bytes 294944 | tf_op jit(solution)/shard_map/ppermute | solution.py:184
  545.0 6.5 %collective-permute-done.48 = bf16[96,768]{1,0:T(8,128)(2,1)S(1)} collective-permute-done((bf16[96,768]{1,0:T(8,128)(2,1)S(1)}, bf16[96,768]{1,0:T(8,128)(2,1)S(1)}, u32[]{:S(2)}, u32[]{:S(2)}) %collective-permute-start.48) | collective-permute-done | bytes 147488 | tf_op jit(solution)/shard_map/ppermute | solution.py:184
  552.2 7.9 %collective-permute-done.38 = bf16[48,1536]{1,0:T(8,128)(2,1)S(1)} collective-permute-done((bf16[48,1536]{1,0:T(8,128)(2,1)S(1)}, bf16[48,1536]{1,0:T(8,128)(2,1)S(1)}, u32[]{:S(2)}, u32[]{:S(2)}) %collective-permute-start.38) | collective-permute-done | bytes 147488 | tf_op jit(solution)/shard_map/ppermute | solution.py:184
  605.1 5.3 dynamic_update_slice.148
  611.7 6.9 %dynamic_update_slice.149 = bf16[384,1152]{0,1:T(8,128)(2,1)S(1)} dynamic-update-slice(bf16[384,1152]{0,1:T(8,128)(2,1)S(1)} %dynamic_update_slice.148, bf16[192,1152]{0,1:T(8,128)(2,1)S(1)} %copy.93, s32[]{:T(128)S(6)} %select_n.214, s32[]{:T(128)} %constant.64.clone.1) | dynamic-update-slice | bytes 884740 | tf_op jit(solution)/shard_map/dynamic_update_slice | solution.py:201
  (409 shorter events, 272.7 us)
Async XLA Ops:
  6.9 39.9 %collective-permute-start = (bf16[384,1152]{0,1:T(8,128)(2,1)}, bf16[384,1152]{0,1:T(8,128)(2,1)}, u32[]{:S(2)}, u32[]{:S(2)}) collective-permute-start(bf16[384,1152]{0,1:T(8,128)(2,1)} %constant_dynamic-slice_fusion.4), channel_id=1, source_target_pairs={{0,1},{1,0},{2,3},{3,2},{4,5},{5,4},{6,7},{7,6},{8,9},{9,8},{10,11... | collective-permute-start | bytes 2654216 | tf_op jit(solution)/shard_map/ppermute | solution.py:179
  11.6 34.1 %collective-permute-start.3 = (bf16[192,768]{1,0:T(8,128)(2,1)}, bf16[192,768]{1,0:T(8,128)(2,1)S(1)}, u32[]{:S(2)}, u32[]{:S(2)}) collective-permute-start(bf16[192,768]{1,0:T(8,128)(2,1)} %constant_dynamic-slice_fusion.3), channel_id=1, source_target_pairs={{0,1},{1,0},{2,3},{3,2},{4,5},{5,4},{6,7},{7,6},{8,9},{9,8},{10,11... | collective-permute-start | bytes 884744 | tf_op jit(solution)/shard_map/ppermute | solution.py:179
  15.9 46.4 %collective-permute-start.5 = (bf16[384,1536]{1,0:T(8,128)(2,1)}, bf16[384,1536]{1,0:T(8,128)(2,1)}, u32[]{:S(2)}, u32[]{:S(2)}) collective-permute-start(bf16[384,1536]{1,0:T(8,128)(2,1)} %constant_dynamic-slice_fusion.2), channel_id=1, source_target_pairs={{0,1},{1,0},{2,3},{3,2},{4,5},{5,4},{6,7},{7,6},{8,9},{9,8},{10,11... | collective-permute-start | bytes 3538952 | tf_op jit(solution)/shard_map/ppermute | solution.py:179
  16.0 111.9 %collective-permute-start.7 = (f32[1536]{0:T(1024)S(1)}, f32[1536]{0:T(1024)S(1)}, u32[]{:S(2)}, u32[]{:S(2)}) collective-permute-start(f32[1536]{0:T(1024)S(1)} %copy-done.44), channel_id=1, source_target_pairs={{0,1},{1,0},{2,3},{3,2},{4,5},{5,4},{6,7},{7,6},{8,9},{9,8},{10,11... | collective-permute-start | bytes 18440 | tf_op jit(solution)/shard_map/ppermute | solution.py:179
  30.7 56.2 %collective-permute-start.8 = (bf16[768,768]{1,0:T(8,128)(2,1)}, bf16[768,768]{1,0:T(8,128)(2,1)S(1)}, u32[]{:S(2)}, u32[]{:S(2)}) collective-permute-start(bf16[768,768]{1,0:T(8,128)(2,1)} %constant_dynamic-slice_fusion.1), channel_id=1, source_target_pairs={{0,1},{1,0},{2,3},{3,2},{4,5},{5,4},{6,7},{7,6},{8,9},{9,8},{10,11... | collective-permute-start | bytes 3538952 | tf_op jit(solution)/shard_map/ppermute | solution.py:179
  46.8 41.8 %collective-permute-start.1 = (bf16[384,1152]{0,1:T(8,128)(2,1)}, bf16[384,1152]{0,1:T(8,128)(2,1)S(1)}, u32[]{:S(2)}, u32[]{:S(2)}) collective-permute-start(bf16[384,1152]{0,1:T(8,128)(2,1)} %collective-permute-done), channel_id=1, source_target_pairs={{0,2},{2,0},{4,6},{6,4},{8,10},{10,8},{12,14},{14,12},{16,18},{18,... | collective-permute-start | bytes 2654216 | tf_op jit(solution)/shard_map/ppermute | solution.py:184
  62.3 65.5 %collective-permute-start.6 = (bf16[384,1536]{1,0:T(8,128)(2,1)}, bf16[384,1536]{1,0:T(8,128)(2,1)S(1)}, u32[]{:S(2)}, u32[]{:S(2)}) collective-permute-start(bf16[384,1536]{1,0:T(8,128)(2,1)} %collective-permute-done.5), channel_id=1, source_target_pairs={{0,2},{2,0},{4,6},{6,4},{8,10},{10,8},{12,14},{14,12},{16,18},{18,... | collective-permute-start | bytes 3538952 | tf_op jit(solution)/shard_map/ppermute | solution.py:184
  86.8 59.5 %collective-permute-start.9 = (bf16[768,768]{1,0:T(8,128)(2,1)S(1)}, bf16[768,768]{1,0:T(8,128)(2,1)S(1)}, u32[]{:S(2)}, u32[]{:S(2)}) collective-permute-start(bf16[768,768]{1,0:T(8,128)(2,1)S(1)} %collective-permute-done.8), channel_id=1, source_target_pairs={{0,2},{2,0},{4,6},{6,4},{8,10},{10,8},{12,14},{14,12},{16,18},{18,... | collective-permute-start | bytes 3538952 | tf_op jit(solution)/shard_map/ppermute | solution.py:184
  245.9 319.9 %collective-permute-start.11 = (bf16[1024,768]{0,1:T(8,128)(2,1)}, bf16[1024,768]{0,1:T(8,128)(2,1)}, u32[]{:S(2)}, u32[]{:S(2)}) collective-permute-start(bf16[1024,768]{0,1:T(8,128)(2,1)} %fusion.47), channel_id=1, source_target_pairs={{0,1},{1,0},{2,3},{3,2},{4,5},{5,4},{6,7},{7,6},{8,9},{9,8},{10,11... | collective-permute-start | bytes 4718600 | tf_op jit(solution)/shard_map/ppermute | solution.py:179
  250.6 192.1 %collective-permute-start.44 = (bf16[768,768]{1,0:T(8,128)(2,1)}, bf16[768,768]{1,0:T(8,128)(2,1)}, u32[]{:S(2)}, u32[]{:S(2)}) collective-permute-start(bf16[768,768]{1,0:T(8,128)(2,1)} %dynamic-slice_convert_fusion), channel_id=1, source_target_pairs={{0,2},{2,0},{4,6},{6,4},{8,10},{10,8},{12,14},{14,12},{16,18},{18,... | collective-permute-start | bytes 3538952 | tf_op jit(solution)/shard_map/ppermute | solution.py:184
  267.6 70.0 %collective-permute-start.23 = (bf16[192,768]{1,0:T(8,128)(2,1)S(1)}, bf16[192,768]{1,0:T(8,128)(2,1)S(1)}, u32[]{:S(2)}, u32[]{:S(2)}) collective-permute-start(bf16[192,768]{1,0:T(8,128)(2,1)S(1)} %dynamic-slice_convert_fusion.12), channel_id=1, source_target_pairs={{0,2},{2,0},{4,6},{6,4},{8,10},{10,8},{12,14},{14,12},{16,18},{18,... | collective-permute-start | bytes 884744 | tf_op jit(solution)/shard_map/ppermute | solution.py:184
  270.5 67.2 %collective-permute-start.25 = (bf16[192,768]{1,0:T(8,128)(2,1)S(1)}, bf16[192,768]{1,0:T(8,128)(2,1)S(1)}, u32[]{:S(2)}, u32[]{:S(2)}) collective-permute-start(bf16[192,768]{1,0:T(8,128)(2,1)S(1)} %add_convert_fusion.3), channel_id=1, source_target_pairs={{0,1},{1,0},{2,3},{3,2},{4,5},{5,4},{6,7},{7,6},{8,9},{9,8},{10,11... | collective-permute-start | bytes 884744 | tf_op jit(solution)/shard_map/ppermute | solution.py:179
  271.0 90.2 %collective-permute-start.13 = (bf16[384,1152]{1,0:T(8,128)(2,1)}, bf16[384,1152]{1,0:T(8,128)(2,1)}, u32[]{:S(2)}, u32[]{:S(2)}) collective-permute-start(bf16[384,1152]{1,0:T(8,128)(2,1)} %dynamic-slice_convert_fusion.4), channel_id=1, source_target_pairs={{0,2},{2,0},{4,6},{6,4},{8,10},{10,8},{12,14},{14,12},{16,18},{18,... | collective-permute-start | bytes 2654216 | tf_op jit(solution)/shard_map/ppermute | solution.py:184
  337.6 108.0 %collective-permute-start.12 = (bf16[384,1152]{1,0:T(8,128)(2,1)S(1)}, bf16[384,1152]{1,0:T(8,128)(2,1)}, u32[]{:S(2)}, u32[]{:S(2)}) collective-permute-start(bf16[384,1152]{1,0:T(8,128)(2,1)S(1)} %dynamic-slice_convert_fusion.5), channel_id=1, source_target_pairs={{0,2},{2,0},{4,6},{6,4},{8,10},{10,8},{12,14},{14,12},{16,18},{18,... | collective-permute-start | bytes 2654216 | tf_op jit(solution)/shard_map/ppermute | solution.py:184
  364.0 81.7 %collective-permute-start.14 = (bf16[384,1152]{1,0:T(8,128)(2,1)}, bf16[384,1152]{1,0:T(8,128)(2,1)}, u32[]{:S(2)}, u32[]{:S(2)}) collective-permute-start(bf16[384,1152]{1,0:T(8,128)(2,1)} %add_convert_fusion.2), channel_id=1, source_target_pairs={{0,1},{1,0},{2,3},{3,2},{4,5},{5,4},{6,7},{7,6},{8,9},{9,8},{10,11... | collective-permute-start | bytes 2654216 | tf_op jit(solution)/shard_map/ppermute | solution.py:179
  381.9 60.6 %collective-permute-start.31 = (bf16[96,768]{1,0:T(8,128)(2,1)S(1)}, bf16[96,768]{1,0:T(8,128)(2,1)S(1)}, u32[]{:S(2)}, u32[]{:S(2)}) collective-permute-start(bf16[96,768]{1,0:T(8,128)(2,1)S(1)} %constant_dynamic-update-slice_fusion.20), channel_id=1, source_target_pairs={{0,4},{2,6},{4,0},{6,2},{8,12},{10,14},{12,8},{14,10},{16,20},{18,... | collective-permute-start | bytes 442376 | tf_op jit(solution)/shard_map/ppermute | solution.py:184
  445.6 30.2 %collective-permute-start.33 = (bf16[384,1536]{1,0:T(8,128)(2,1)}, bf16[384,1536]{1,0:T(8,128)(2,1)S(1)}, u32[]{:S(2)}, u32[]{:S(2)}) collective-permute-start(bf16[384,1536]{1,0:T(8,128)(2,1)} %dynamic-slice_convert_fusion.3), channel_id=1, source_target_pairs={{0,2},{2,0},{4,6},{6,4},{8,10},{10,8},{12,14},{14,12},{16,18},{18,... | collective-permute-start | bytes 3538952 | tf_op jit(solution)/shard_map/ppermute | solution.py:184
  461.0 38.9 %collective-permute-start.35 = (bf16[384,1536]{1,0:T(8,128)(2,1)S(1)}, bf16[384,1536]{1,0:T(8,128)(2,1)S(1)}, u32[]{:S(2)}, u32[]{:S(2)}) collective-permute-start(bf16[384,1536]{1,0:T(8,128)(2,1)S(1)} %add_convert_fusion.1), channel_id=1, source_target_pairs={{0,1},{1,0},{2,3},{3,2},{4,5},{5,4},{6,7},{7,6},{8,9},{9,8},{10,11... | collective-permute-start | bytes 3538952 | tf_op jit(solution)/shard_map/ppermute | solution.py:179
  462.6 140.6 %collective-permute-start.10 = (bf16[1024,768]{0,1:T(8,128)(2,1)}, bf16[1024,768]{0,1:T(8,128)(2,1)}, u32[]{:S(2)}, u32[]{:S(2)}) collective-permute-start(bf16[1024,768]{0,1:T(8,128)(2,1)} %get-tuple-element.104), channel_id=1, source_target_pairs={{0,1},{1,0},{2,3},{3,2},{4,5},{5,4},{6,7},{7,6},{8,9},{9,8},{10,11... | collective-permute-start | bytes 4718600 | tf_op jit(solution)/shard_map/ppermute | solution.py:179
  475.8 42.4 %collective-permute-start.46 = (bf16[384,768]{1,0:T(8,128)(2,1)}, bf16[384,768]{1,0:T(8,128)(2,1)}, u32[]{:S(2)}, u32[]{:S(2)}) collective-permute-start(bf16[384,768]{1,0:T(8,128)(2,1)} %dynamic-slice_convert_fusion.6), channel_id=1, source_target_pairs={{0,4},{2,6},{4,0},{6,2},{8,12},{10,14},{12,8},{14,10},{16,20},{18,... | collective-permute-start | bytes 1769480 | tf_op jit(solution)/shard_map/ppermute | solution.py:184
  513.6 47.2 %collective-permute-start.32 = (bf16[192,768]{1,0:T(8,128)(2,1)}, bf16[192,768]{1,0:T(8,128)(2,1)}, u32[]{:S(2)}, u32[]{:S(2)}) collective-permute-start(bf16[192,768]{1,0:T(8,128)(2,1)} %copy-done.33), channel_id=1, source_target_pairs={{0,2},{2,0},{4,6},{6,4},{8,10},{10,8},{12,14},{14,12},{16,18},{18,... | collective-permute-start | bytes 884744 | tf_op jit(solution)/shard_map/ppermute | solution.py:184
  518.2 55.5 %collective-permute-start.19 = (bf16[96,1152]{0,1:T(8,128)(2,1)}, bf16[96,1152]{0,1:T(8,128)(2,1)}, u32[]{:S(2)}, u32[]{:S(2)}) collective-permute-start(bf16[96,1152]{0,1:T(8,128)(2,1)} %dynamic_update_slice.145), channel_id=1, source_target_pairs={{0,8},{2,10},{4,12},{6,14},{8,0},{10,2},{12,4},{14,6},{16,24},{18,... | collective-permute-start | bytes 663560 | tf_op jit(solution)/shard_map/ppermute | solution.py:184
  580.9 29.6 %collective-permute-start.20 = (bf16[192,1152]{1,0:T(8,128)(2,1)}, bf16[192,1152]{1,0:T(8,128)(2,1)}, u32[]{:S(2)}, u32[]{:S(2)}) collective-permute-start(bf16[192,1152]{1,0:T(8,128)(2,1)} %copy.92), channel_id=1, source_target_pairs={{0,4},{2,6},{4,0},{6,2},{8,12},{10,14},{12,8},{14,10},{16,20},{18,... | collective-permute-start | bytes 1327112 | tf_op jit(solution)/shard_map/ppermute | solution.py:184
  593.4 31.4 %collective-permute-start.51 = (bf16[384,768]{1,0:T(8,128)(2,1)}, bf16[384,768]{1,0:T(8,128)(2,1)}, u32[]{:S(2)}, u32[]{:S(2)}) collective-permute-start(bf16[384,768]{1,0:T(8,128)(2,1)} %constant_dynamic-update-slice_fusion.4), channel_id=1, source_target_pairs={{0,4},{2,6},{4,0},{6,2},{8,12},{10,14},{12,8},{14,10},{16,20},{18,... | collective-permute-start | bytes 1769480 | tf_op jit(solution)/shard_map/ppermute | solution.py:184
  (86 other events, 961.6 us)
